TPU v7x, 32 devices: a whole 2x2x4 slice. The times are simulated.
32 devices in a mesh: dp: 2 (over x), ep: 16 (over z, y, core).
Axes of the slice: x: 2, y: 2, z: 4, core: 2. Of those that a mesh axis runs over, the one named last changes fastest.
Arguments:
- queries: bfloat16 [2048, 36864], P('ep', 'dp'), may hold values from -40 to 40
- suffix_latent: bfloat16 [2048, 576], P('ep'), may hold values from -10 to 10
- page_pool: bfloat16 [128, 36864], P('ep'), may hold values from -6 to 6
- page_owner: int32 [16, 32], P('ep'), may hold values from 0 to 15, as said below
- page_slot: int32 [16, 32], P('ep'), may hold values from 0 to 7
- prefix_len: int32 [16], P('ep'), may hold values from 1025 to 2048, as said below
- moe_input: bfloat16 [512, 3584], P(('dp', 'ep')), may hold values from -6 to 6
- expert_ids: int32 [512, 8], P(('dp', 'ep')), may hold values from 0 to 15, all different within a row; in each aligned block of 16 rows (0 to 15, 16 to 31, ...) at most 10 rows name the same one
- gate_weights: float32 [512, 8], P(('dp', 'ep')), may hold values from 0.1 to 0.6
- w_gate: bfloat16 [16, 3584, 1024], P('ep', None, 'dp'), may hold values from -0.09375 to 0.09375
- w_up: bfloat16 [16, 3584, 1024], P('ep', None, 'dp'), may hold values from -0.09375 to 0.09375
- w_down: bfloat16 [16, 1024, 3584], P('ep', 'dp'), may hold values from -0.1875 to 0.1875
Outputs:
- attn_context: bfloat16 [2048, 32768], P('ep', 'dp')
- moe_output: bfloat16 [512, 3584], P(('dp', 'ep'))
Inputs may be any that keep to these rules, and one draw needn't show every extreme that they name: `page_owner`: for a multiple m of the ep axis's size, the pages m, m + 1, ... of one request up to m + that size - 1 have distinct owners, so page k is the (k div that size)-th page of its request on its owner; entries past a request's prefix are valid page references too. `prefix_len`: some request has the longest prefix, 2048 tokens. `expert_ids`: in the 16 rows of one device no expert is named by more than 10 rows.
All inputs are finite; a program needn't handle non-finite values.
Results may differ from a plain program's by a relative error of at most 0.0057.
Values may be sent and summed in bfloat16 or wider, within the bound.
No kernel may reach another device: no remote copies, remote signals or barrier semaphores. Data moves between devices by JAX's collectives and lax.ppermute only.
A program may use at most 192 MiB of HBM per device.

v0:
```python
import jax
import jax.numpy as jnp
from jax import lax
from jax.sharding import PartitionSpec as P

LATENT = 512
ROPE = 64
PAGE = 64
score_scale = 0.07216878364870322
neg_large = -1e30


def attend(query_rows, suffix_rows, prefix_keys, length):
    new_tokens = suffix_rows.shape[0]
    key_width = suffix_rows.shape[1]
    head_count = query_rows.shape[1] // key_width
    flat_queries = query_rows.reshape(new_tokens * head_count, key_width)
    all_keys = jnp.concatenate([prefix_keys, suffix_rows], axis=0)
    scores = (
        lax.dot_general(
            flat_queries, all_keys, (((1,), (1,)), ((), ())), preferred_element_type=jnp.float32
        )
        * score_scale
    )
    prefix_count = prefix_keys.shape[0]
    key_index = jnp.arange(prefix_count + new_tokens, dtype=jnp.int32)[None, :]
    row_token = (jnp.arange(new_tokens * head_count, dtype=jnp.int32) // head_count)[:, None]
    allowed = jnp.where(
        key_index < prefix_count, key_index < length, key_index - prefix_count <= row_token
    )
    masked = jnp.where(allowed, scores, neg_large)
    row_max = jnp.max(masked, axis=1, keepdims=True)
    exponent = jnp.where(allowed, jnp.exp(masked - row_max), 0.0)
    probs = (exponent / jnp.sum(exponent, axis=1, keepdims=True)).astype(jnp.bfloat16)
    context = jnp.dot(probs, all_keys[:, :LATENT], preferred_element_type=jnp.float32)
    return context.astype(jnp.bfloat16).reshape(new_tokens, head_count * LATENT)


def slot_table(owners, slot_ids, targets, slot_count, stride):
    page_rank = jnp.arange(owners.shape[1], dtype=jnp.int32) // stride
    slot_range = jnp.arange(slot_count, dtype=jnp.int32)
    matches = (owners[:, None, None, :] == targets[None, :, None, None]) & (
        page_rank[None, None, None, :] == slot_range[None, None, :, None]
    )
    return jnp.sum(jnp.where(matches, slot_ids[:, None, None, :], 0), axis=3)


def fetch_pages(page_pool, page_owner, page_slot):
    ep_size = lax.axis_size("ep")
    page_total = page_owner.shape[1]
    slot_count = (page_total + ep_size - 1) // ep_size
    everyone = jnp.arange(ep_size, dtype=jnp.int32)
    wanted = slot_table(page_owner, page_slot, everyone, slot_count, ep_size)[0]
    fetched = lax.all_to_all(
        page_pool[lax.all_to_all(wanted, "ep", split_axis=0, concat_axis=0, tiled=True)],
        "ep",
        split_axis=0,
        concat_axis=0,
        tiled=True,
    )
    flat_rows = fetched.reshape(ep_size * slot_count, fetched.shape[2])
    page_order = page_owner[0] * slot_count + jnp.arange(page_total, dtype=jnp.int32) // ep_size
    return flat_rows[page_order].reshape(page_total * PAGE, LATENT + ROPE)


def experts_part(moe_input, expert_ids, gate_weights, w_gate, w_up, w_down):
    ep_size = lax.axis_size("ep")
    tok_count, top_count = expert_ids.shape
    capacity = min(tok_count, max(2, 5 * tok_count * top_count // (4 * ep_size)))
    features = moe_input.shape[1]
    flat_ids = expert_ids.reshape(tok_count * top_count)
    onehot = (flat_ids[:, None] == jnp.arange(ep_size, dtype=jnp.int32)[None, :]).astype(jnp.int32)
    slot_index = jnp.sum((jnp.cumsum(onehot, axis=0) - 1) * onehot, axis=1)
    target = (flat_ids * capacity + slot_index).reshape(tok_count, top_count)
    cells = jnp.arange(ep_size * capacity, dtype=jnp.int32)
    placed = jnp.any(target[None, :, :] == cells[:, None, None], axis=2).astype(jnp.bfloat16)
    outgoing = jnp.dot(placed, moe_input, preferred_element_type=jnp.float32).astype(jnp.bfloat16)
    incoming = lax.all_to_all(
        outgoing.reshape(ep_size, capacity, features), "ep", split_axis=0, concat_axis=0, tiled=True
    )
    incoming = incoming.reshape(ep_size * capacity, features)
    gate_local = w_gate[0]
    up_local = w_up[0]
    down_local = w_down[0]
    shard_part = lax.all_gather(incoming, "dp", axis=0, tiled=True)
    gate_proj = jnp.dot(shard_part, gate_local, preferred_element_type=jnp.float32)
    up_proj = jnp.dot(shard_part, up_local, preferred_element_type=jnp.float32)
    hidden_all = (jax.nn.silu(gate_proj) * up_proj).astype(jnp.bfloat16)
    result = lax.psum_scatter(
        jnp.dot(hidden_all, down_local, preferred_element_type=jnp.float32),
        "dp",
        scatter_dimension=0,
        tiled=True,
    )
    returned = lax.all_to_all(
        result.astype(jnp.bfloat16).reshape(ep_size, capacity, features),
        "ep",
        split_axis=0,
        concat_axis=0,
        tiled=True,
    )
    returned = returned.reshape(ep_size * capacity, features)
    picked = returned[target].astype(jnp.float32)
    return jnp.sum(picked * gate_weights[:, :, None], axis=1).astype(jnp.bfloat16)


def on_device(
    queries,
    suffix_latent,
    page_pool,
    page_owner,
    page_slot,
    prefix_len,
    moe_input,
    expert_ids,
    gate_weights,
    w_gate,
    w_up,
    w_down,
):
    prefix_keys = fetch_pages(page_pool, page_owner, page_slot)
    moe_output = experts_part(moe_input, expert_ids, gate_weights, w_gate, w_up, w_down)
    attn_context = attend(queries, suffix_latent, prefix_keys, prefix_len[0])
    return (attn_context, moe_output)


def solution(mesh):
    return jax.shard_map(
        on_device,
        mesh=mesh,
        in_specs=(
            P("ep", "dp"),
            P("ep", None),
            P("ep", None),
            P("ep", None),
            P("ep", None),
            P("ep"),
            P(("dp", "ep"), None),
            P(("dp", "ep"), None),
            P(("dp", "ep"), None),
            P("ep", None, "dp"),
            P("ep", None, "dp"),
            P("ep", "dp", None),
        ),
        out_specs=(P("ep", "dp"), P(("dp", "ep"), None)),
        check_vma=False,
    )
```

profile of v0, /device:TPU:15, one launch (start us, length us, event | category | flops | bytes accessed | tf_op | source)
XLA Modules:
  0.0 267.8 jit_solution(14442339165964018494)
XLA Ops:
  7.2 0.0 copy-start
  7.2 0.0 all-gather.2.cloned.1.call-start
  7.2 0.8 copy.35
  8.0 0.1 eq.73
  8.1 0.1 fusion.32
  8.2 0.2 reduce_window_sum.11
  8.4 0.2 select_reduce_fusion
  8.6 0.1 reduce_sum.41
  8.7 0.1 fusion.31
  8.8 2.4 convolution_convert_fusion
  11.2 1.5 reshape.242
  12.7 0.0 copy-start.6
  12.7 0.0 copy-start.7
  12.7 48.1 %all_to_all.27 = bf16[16,10,3584]{2,1,0:T(8,128)(2,1)} all-to-all(bf16[16,10,3584]{2,1,0:T(8,128)(2,1)S(1)} %reshape.242), channel_id=1, replica_groups=mesh['dp'=2,'ep'=16] {'ep'}, dimensions={0} | all-to-all | bytes 2293760 | tf_op jit(solution)/shard_map/all_to_all | solution.py:78
  60.8 2.5 reshape.243
  63.3 0.0 all-gather.2.cloned.1.call-update
  63.3 0.0 copy-done.6
  63.3 0.0 copy-done.7
  63.3 0.1 select_reduce_fusion.1
  63.5 0.1 copy.31
  63.5 8.6 %all_to_all.28 = s32[16,1,2]{2,1,0:T(1,128)S(1)} all-to-all(s32[16,1,2]{2,1,0:T(1,128)S(1)} %copy.31), channel_id=1, replica_groups=mesh['dp'=2,'ep'=16] {'ep'}, dimensions={0} | all-to-all | bytes 256 | tf_op jit(solution)/shard_map/all_to_all | solution.py:55
  72.2 0.1 copy.32
  72.3 0.1 copy.33
  72.4 0.1 reshape.248
  72.5 0.0 copy-done
  72.5 2.1 gather_fusion
  74.6 2.8 %reshape.247 = bf16[16,2,36864]{2,1,0:T(2,128)(2,1)} reshape(bf16[32,36864]{1,0:T(8,128)(2,1)S(1)} %gather_fusion) | data formatting | bytes 4718592 | tf_op jit(solution)/shard_map/gather | solution.py:55
  77.4 6.9 %all-to-all-start.1 = ((bf16[16,2,36864]{2,1,0:T(2,128)(2,1)}), bf16[16,2,36864]{2,1,0:T(2,128)(2,1)}, u32[]{:S(2)}, u32[]{:S(2)}) async-start(bf16[16,2,36864]{2,1,0:T(2,128)(2,1)} %reshape.247), calls=%async_computation.1 | async-start | bytes 4718592 | tf_op jit(solution)/shard_map/all_to_all | solution.py:54
  84.2 0.0 reduce-scatter.2.cloned.1.call-start
  84.3 13.0 %all-gather.2.cloned.1.call-done = bf16[320,3584]{1,0:T(8,128)(2,1)} async-done(((bf16[160,3584]{1,0:T(8,128)(2,1)}), bf16[320,3584]{1,0:T(8,128)(2,1)}) %all-gather.2.cloned.1.call-update) | async-done | bytes 2293776 | tf_op jit(solution)/shard_map/all_gather | solution.py:85
  97.3 5.1 %fusion.7 = f32[320,512]{1,0:T(8,128)} fusion(bf16[320,3584]{1,0:T(8,128)(2,1)} %all-gather.2.cloned.1.call-done, bf16[1,3584,512]{2,1,0:T(8,128)(2,1)} %param.21), kind=kOutput, calls=%fused_computation.15 | convolution fusion | flops 1174405120 | bytes 6619136 | tf_op jit(solution)/shard_map/dot_general | solution.py:86
  102.3 0.0 copy-done.8
  102.3 8.1 %fusion.3 = f32[320,3584]{1,0:T(8,128)} fusion(bf16[1,512,3584]{2,1,0:T(8,128)(2,1)} %param.23, bf16[320,3584]{1,0:T(8,128)(2,1)S(1)} %copy-done.8, bf16[1,3584,512]{2,1,0:T(8,128)(2,1)} %param.22, f32[320,512]{1,0:T(8,128)} %fusion.7), kind=kOutput, calls=%fused_computation.11 | convolution fusion | flops 2349793280 | bytes 14876672 | tf_op jit(solution)/shard_map/dot_general | solution.py:90
  110.4 0.0 copy-start.4
  110.4 0.0 reduce-scatter.2.cloned.1.call-update
  111.1 0.2 copy-done.4
  111.4 0.2 copy.34
  111.5 0.0 copy-start.5
  111.5 10.1 %reshape.240 = bf16[4096,576]{1,0:T(8,128)(2,1)} reshape(bf16[128,18432]{1,0:T(8,128)(2,1)} %param.12) | data formatting | bytes 9437184 | tf_op jit(solution)/shard_map/reshape | solution.py:17
  121.6 0.1 reshape.264
  121.7 0.0 copy-done.5
  121.7 0.1 copy.37
  121.8 15.8 %all-to-all-done.1 = bf16[16,2,36864]{2,1,0:T(2,128)(2,1)} async-done(((bf16[16,2,36864]{2,1,0:T(2,128)(2,1)}), bf16[16,2,36864]{2,1,0:T(2,128)(2,1)}, u32[]{:S(2)}, u32[]{:S(2)}) %all-to-all-start.1) | async-done | bytes 2359328 | tf_op jit(solution)/shard_map/all_to_all | solution.py:54
  137.7 3.0 %reshape.238 = bf16[32,36864]{1,0:T(8,128)(2,1)S(1)} reshape(bf16[16,2,36864]{2,1,0:T(2,128)(2,1)} %all-to-all-done.1) | data formatting | bytes 4718592 | tf_op jit(solution)/shard_map/reshape | solution.py:61
  140.7 3.5 %gather_fusion.1 = bf16[32,36864]{1,0:T(8,128)(2,1)} fusion(bf16[32,36864]{1,0:T(8,128)(2,1)S(1)} %reshape.238, s32[1024]{0:T(1024)S(1)} %pad_clamp_fusion.1), kind=kCustom, calls=%fused_computation.1 | custom fusion | bytes 4718720 | tf_op jit(solution)/shard_map/gather | solution.py:63
  144.2 4.6 %reshape.239 = bf16[2048,576]{1,0:T(8,128)(2,1)S(1)} reshape(bf16[32,36864]{1,0:T(8,128)(2,1)} %gather_fusion.1) | data formatting | bytes 4718592 | tf_op jit(solution)/shard_map/reshape | solution.py:63
  148.8 0.0 copy-start.2
  148.8 25.5 %fusion = (f32[4096]{0:T(1024)S(1)}, f32[2176,4096]{1,0:T(8,128)}) fusion(s32[4096]{0:T(1024)S(1)} %add_select_fusion, s32[2176]{0:T(1024)S(1)} %iota_add_fusion, pred[2176]{0:T(1024)(128)(4,1)S(1)} %get-tuple-element.8, pred[2176]{0:T(1024)(128)(4,1)S(1)} %get-tuple-element.9, bf16[4096,576]{1,0:T(8,128)(2,1)} %reshape.240, bf16[128,576]{1,0:T(8,128)(2,1)S(1)} %copy.34, ...), kind=kOutput, calls=%fused_computation.7 | convolution fusion | flops 10317230080 | bytes 42922752 | tf_op jit(solution)/shard_map/dot_general | solution.py:20
  174.3 0.0 copy-done.2
  174.3 32.7 %fusion.41 = (f32[4096]{0:T(1024)S(1)}, f32[4096,2176]{0,1:T(8,128)}) fusion(f32[4096]{0:T(1024)S(1)} %get-tuple-element.6, f32[2176,4096]{1,0:T(8,128)} %get-tuple-element.7, s32[4096]{0:T(1024)S(1)} %add_select_fusion, s32[2176]{0:T(1024)S(1)} %iota_add_fusion, pred[2176]{0:T(1024)(128)(4,1)S(1)} %get-tuple-element.8, pred[2176]{0:T(1024)(128)(4,1)S(1)} %get-tuple-element.9), kind=kLoop, calls=%fused_computation.72 | loop fusion | flops 62386176 | bytes 71365376 | tf_op jit(solution)/shard_map/reduce_sum | solution.py:34
  207.0 0.0 reduce-scatter.2.cloned.1.call-done
  207.0 1.8 convert_element_type.30
  208.8 1.5 reshape.244
  210.2 0.0 copy-start.3
  210.2 4.8 %all-to-all-start.3 = ((bf16[16,10,3584]{2,1,0:T(8,128)(2,1)}), bf16[16,10,3584]{2,1,0:T(8,128)(2,1)}, u32[]{:S(2)}, u32[]{:S(2)}) async-start(bf16[16,10,3584]{2,1,0:T(8,128)(2,1)} %reshape.244), calls=%async_computation.4 | async-start | bytes 3670016 | tf_op jit(solution)/shard_map/all_to_all | solution.py:95
  215.0 0.0 copy-done.3
  215.0 17.7 %fusion.2 = bf16[4096,512]{1,0:T(8,128)(2,1)} fusion(f32[4096,2176]{0,1:T(8,128)} %get-tuple-element.5, f32[4096]{0:T(1024)S(1)} %get-tuple-element.4, bf16[128,576]{1,0:T(8,128)(2,1)S(1)} %copy.34, bf16[2048,576]{1,0:T(8,128)(2,1)S(1)} %copy-done.3), kind=kOutput, calls=%fused_computation.9 | convolution fusion | flops 9151184896 | bytes 42369024 | tf_op jit(solution)/shard_map/dot_general | solution.py:35
  232.7 7.4 %reshape.241 = bf16[128,16384]{1,0:T(8,128)(2,1)} reshape(bf16[4096,512]{1,0:T(8,128)(2,1)} %fusion.2) | data formatting | bytes 8388608 | tf_op jit(solution)/shard_map/reshape | solution.py:36
  240.1 16.6 %all-to-all-done.3 = bf16[16,10,3584]{2,1,0:T(8,128)(2,1)} async-done(((bf16[16,10,3584]{2,1,0:T(8,128)(2,1)}), bf16[16,10,3584]{2,1,0:T(8,128)(2,1)}, u32[]{:S(2)}, u32[]{:S(2)}) %all-to-all-start.3) | async-done | bytes 1146912 | tf_op jit(solution)/shard_map/all_to_all | solution.py:95
  256.7 0.0 copy-start.1
  256.7 1.7 reshape.245
  258.5 1.1 gather_fusion.2
  259.6 1.3 fusion.16
  260.9 0.0 copy-done.1
  (13 shorter events, 0.1 us)
Async XLA Ops:
  7.2 65.3 %copy-start = (bf16[8,36864]{1,0:T(8,128)(2,1)S(1)}, bf16[8,36864]{1,0:T(8,128)(2,1)}, u32[]{:S(2)}) copy-start(bf16[8,36864]{1,0:T(8,128)(2,1)} %param.14) | copy-start | bytes 1769476
  7.2 90.1 %all-gather.2.cloned.1.call-start = ((), (), s32[]{:S(2)}) async-start(), calls=%async_computation.5 | async-start | bytes 3440640 | tf_op jit(solution)/shard_map/all_gather | solution.py:85
  12.7 50.6 %copy-start.6 = (s32[1,32]{1,0:T(1,128)S(1)}, s32[1,32]{1,0:T(1,128)}, u32[]{:S(2)}) copy-start(s32[1,32]{1,0:T(1,128)} %param.15) | copy-start | bytes 388
  12.7 50.6 %copy-start.7 = (s32[1,32]{1,0:T(1,128)S(1)}, s32[1,32]{1,0:T(1,128)}, u32[]{:S(2)}) copy-start(s32[1,32]{1,0:T(1,128)} %param.16) | copy-start | bytes 388
  77.4 60.3 %all-to-all-start.1 = ((bf16[16,2,36864]{2,1,0:T(2,128)(2,1)}), bf16[16,2,36864]{2,1,0:T(2,128)(2,1)}, u32[]{:S(2)}, u32[]{:S(2)}) async-start(bf16[16,2,36864]{2,1,0:T(2,128)(2,1)} %reshape.247), calls=%async_computation.1 | async-start | bytes 4718592 | tf_op jit(solution)/shard_map/all_to_all | solution.py:54
  84.2 122.8 %reduce-scatter.2.cloned.1.call-start = ((), (), s32[]{:S(2)}) async-start(), calls=%async_computation.6 | async-start | bytes 6881280 | tf_op jit(solution)/shard_map/reduce_scatter | solution.py:89
  97.3 5.1 %copy-start.8 = (bf16[320,3584]{1,0:T(8,128)(2,1)S(1)}, bf16[320,3584]{1,0:T(8,128)(2,1)}, u32[]{:S(2)}) copy-start(bf16[320,3584]{1,0:T(8,128)(2,1)} %all-gather.2.cloned.1.call-done) | copy-start | bytes 6881284
  110.4 0.9 copy-start.4
  111.5 10.2 %copy-start.5 = (f32[16,8]{0,1:T(8,128)S(1)}, f32[16,8]{0,1:T(8,128)}, u32[]{:S(2)}) copy-start(f32[16,8]{0,1:T(8,128)} %param.20) | copy-start | bytes 1540
  148.8 25.5 %copy-start.2 = (bf16[2048,576]{1,0:T(8,128)(2,1)}, bf16[2048,576]{1,0:T(8,128)(2,1)S(1)}, u32[]{:S(2)}) copy-start(bf16[2048,576]{1,0:T(8,128)(2,1)S(1)} %reshape.239) | copy-start | bytes 7077892
  210.2 4.8 %copy-start.3 = (bf16[2048,576]{1,0:T(8,128)(2,1)S(1)}, bf16[2048,576]{1,0:T(8,128)(2,1)}, u32[]{:S(2)}) copy-start(bf16[2048,576]{1,0:T(8,128)(2,1)} %copy-done.2) | copy-start | bytes 7077892
  210.2 46.5 %all-to-all-start.3 = ((bf16[16,10,3584]{2,1,0:T(8,128)(2,1)}), bf16[16,10,3584]{2,1,0:T(8,128)(2,1)}, u32[]{:S(2)}, u32[]{:S(2)}) async-start(bf16[16,10,3584]{2,1,0:T(8,128)(2,1)} %reshape.244), calls=%async_computation.4 | async-start | bytes 3670016 | tf_op jit(solution)/shard_map/all_to_all | solution.py:95
  256.7 4.2 %copy-start.1 = (bf16[8,36864]{1,0:T(8,128)(2,1)S(1)}, bf16[8,36864]{1,0:T(8,128)(2,1)}, u32[]{:S(2)}) copy-start(bf16[8,36864]{1,0:T(8,128)(2,1)} %param.14) | copy-start | bytes 1769476
Sparse Core Ops, SparseCore 0:
  63.4 33.8 all-gather.1
  110.6 58.6 reduce-scatter.1
where the time goes:
time: 269 us; the launch traced here: 268 us
  matrix products  58.7 us (22%)
  blocking collectives  56.7 us (21%)
  waiting for transfers between devices  45.5 us (17%)
  local copies, waits for them, and re-layouts  43.5 us (16%)
  other arithmetic  36.6 us (14%)
  between operations  15 us (6%)
  starting transfers between devices  11.8 us (4%)
    all_to_all x1, blocking collectives, experts_part(): lax.all_to_all(outgoing.reshape(ep_size, capacity, features), 'ep', split...  48.1 us
    reduce_sum x1, other arithmetic, attend(): jnp.sum(exponent, axis=1, keepdims=True)  32.7 us
    dot_general x1, matrix products, attend(): lax.dot_general(flat_queries, all_keys, (((1,), (1,)), ((), ())), preferr...  25.5 us
    dot_general x1, matrix products, attend(): jnp.dot(probs, all_keys[:, :LATENT], preferred_element_type=jnp.float32)  17.7 us
    all_to_all x1, waiting for transfers between devices, experts_part(): lax.all_to_all(result.astype(jnp.bfloat16).reshape(ep_size, capacity, fea...  16.6 us
    all_to_all x1, waiting for transfers between devices, fetch_pages(): lax.all_to_all(page_pool[lax.all_to_all(wanted, 'ep', split_axis=0, conca...  15.8 us
    all_gather x1, waiting for transfers between devices, experts_part(): shard_part = lax.all_gather(incoming, 'dp', axis=0, tiled=True)  13 us
    reshape x1, local copies, waits for them, and re-layouts, attend(): flat_queries = query_rows.reshape(new_tokens * head_count, key_width)  10.1 us
  transfers between devices with their start and end apart: 4, of which 3 were waited for; matrix products, arithmetic and copies ran while one was open for 46% of the time, Pallas kernels for 0%

commit v1 on v0

--- a/solution.py
+++ b/solution.py
@@ -51,13 +51,19 @@
     slot_count = (page_total + ep_size - 1) // ep_size
     everyone = jnp.arange(ep_size, dtype=jnp.int32)
     wanted = slot_table(page_owner, page_slot, everyone, slot_count, ep_size)[0]
-    fetched = lax.all_to_all(
-        page_pool[lax.all_to_all(wanted, "ep", split_axis=0, concat_axis=0, tiled=True)],
-        "ep",
-        split_axis=0,
-        concat_axis=0,
-        tiled=True,
-    )
+    x = page_pool[lax.all_to_all(wanted, "ep", split_axis=0, concat_axis=0, tiled=True)]
+    ways, here = (lax.axis_size("ep"), lax.axis_index("ep"))
+    width = x.shape[0] // ways
+    dims = list(x.shape)
+    dims[0] = width
+    height = dims[0]
+    dims[0] = height * ways
+    fetched = jnp.zeros(dims, x.dtype)
+    for mask in range(ways):
+        part = lax.dynamic_slice_in_dim(x, (here ^ mask) * width, width, axis=0)
+        if mask:
+            part = lax.ppermute(part, "ep", [(d, d ^ mask) for d in range(ways)])
+        fetched = lax.dynamic_update_slice_in_dim(fetched, part, (here ^ mask) * height, axis=0)
     flat_rows = fetched.reshape(ep_size * slot_count, fetched.shape[2])
     page_order = page_owner[0] * slot_count + jnp.arange(page_total, dtype=jnp.int32) // ep_size
     return flat_rows[page_order].reshape(page_total * PAGE, LATENT + ROPE)

time: 269 us -> 299 us (1.11)
  blocking collectives: 56.7 us -> 0 us
  waiting for transfers between devices: 45.5 us -> 83.7 us
  starting transfers between devices: 11.8 us -> 41.3 us
  local copies, waits for them, and re-layouts: 43.5 us -> 61.2 us
    all_to_all x2 -> x0, blocking collectives: 56.7 us -> none  [the longest x1 48.1 us: experts_part(): lax.all_to_all(outgoing.reshape(ep_size, capacity, features), 'ep', split...]
    ppermute x0 -> x15, waiting for transfers between devices: none -> 34.3 us  [fetch_pages(): part = lax.ppermute(part, 'ep', [(d, d ^ mask) for d in range(ways)])]
    ppermute x0 -> x15, starting transfers between devices: none -> 21.8 us  [fetch_pages(): part = lax.ppermute(part, 'ep', [(d, d ^ mask) for d in range(ways)])]
    all_gather x1, waiting for transfers between devices: 13 us -> 32.5 us  [experts_part(): shard_part = lax.all_gather(incoming, 'dp', axis=0, tiled=True)]
    all_to_all x1 -> x2, waiting for transfers between devices: 15.8 us -> 0.01 us  [the longest x1 0.01 us: fetch_pages(): lax.all_to_all(wanted, 'ep', split_axis=0, concat_axis=0, tiled=True)]
    dynamic_update_slice x0 -> x15, local copies, waits for them, and re-layouts: none -> 11.5 us  [fetch_pages(): lax.dynamic_update_slice_in_dim(fetched, part, (here ^ mask) * height, ax...]
    all_to_all x1 -> x2, starting transfers between devices: 6.88 us -> 12.6 us  [the longest x1 6.52 us: fetch_pages(): lax.all_to_all(wanted, 'ep', split_axis=0, concat_axis=0, tiled=True)]
    broadcast_in_dim x0 -> x1, local copies, waits for them, and re-layouts: none -> 3.23 us  [fetch_pages(): fetched = jnp.zeros(dims, x.dtype)]
  transfers between devices with their start and end apart: 4 -> 20, of which waited for: 3 -> 9; matrix products, arithmetic and copies ran while one was open for 46% -> 50% of each run, Pallas kernels for 0% -> 0%
where the time goes in v1:
time: 299 us; the launch traced here: 297 us
  waiting for transfers between devices  83.7 us (28%)
  local copies, waits for them, and re-layouts  61.2 us (20%)
  matrix products  57.2 us (19%)
  starting transfers between devices  41.3 us (14%)
  other arithmetic  38.6 us (13%)
  between operations  15 us (5%)
    ppermute x15, waiting for transfers between devices, fetch_pages(): part = lax.ppermute(part, 'ep', [(d, d ^ mask) for d in range(ways)])  34.3 us
    reduce_sum x1, other arithmetic, attend(): jnp.sum(exponent, axis=1, keepdims=True)  32.7 us
    all_gather x1, waiting for transfers between devices, experts_part(): shard_part = lax.all_gather(incoming, 'dp', axis=0, tiled=True)  32.5 us
    dot_general x1, matrix products, attend(): lax.dot_general(flat_queries, all_keys, (((1,), (1,)), ((), ())), preferr...  25.5 us
    ppermute x15, starting transfers between devices, fetch_pages(): part = lax.ppermute(part, 'ep', [(d, d ^ mask) for d in range(ways)])  21.8 us
    dot_general x1, matrix products, attend(): jnp.dot(probs, all_keys[:, :LATENT], preferred_element_type=jnp.float32)  17.7 us
    all_to_all x1, waiting for transfers between devices, experts_part(): lax.all_to_all(result.astype(jnp.bfloat16).reshape(ep_size, capacity, fea...  16.9 us
    dynamic_update_slice x15, local copies, waits for them, and re-layouts, fetch_pages(): lax.dynamic_update_slice_in_dim(fetched, part, (here ^ mask) * height, ax...  11.5 us
  transfers between devices with their start and end apart: 20, of which 9 were waited for; matrix products, arithmetic and copies ran while one was open for 50% of the time, Pallas kernels for 0%

profile of v1, /device:TPU:15, one launch (start us, length us, event | category | flops | bytes accessed | tf_op | source)
XLA Modules:
  0.0 297.0 jit_solution(3773336234411104104)
XLA Ops:
  7.2 0.7 iota_compare_fusion.4
  7.9 0.8 select_reduce_fusion.1
  8.7 0.7 copy.31
  9.4 6.5 %all-to-all-start = ((s32[16,1,2]{2,1,0:T(1,128)}), s32[16,1,2]{2,1,0:T(1,128)S(1)}, u32[]{:S(2)}, u32[]{:S(2)}) async-start(s32[16,1,2]{2,1,0:T(1,128)} %copy.31), calls=%async_computation | async-start | bytes 16384 | tf_op jit(solution)/shard_map/all_to_all | solution.py:54
  15.9 0.7 fusion.37
  17.2 0.8 copy.35
  18.8 1.4 convolution_convert_fusion
  20.2 1.4 reshape.242
  21.8 6.0 %all-to-all-start.1 = ((bf16[16,10,3584]{2,1,0:T(8,128)(2,1)}), bf16[16,10,3584]{2,1,0:T(8,128)(2,1)}, u32[]{:S(2)}, u32[]{:S(2)}) async-start(bf16[16,10,3584]{2,1,0:T(8,128)(2,1)} %reshape.242), calls=%async_computation.1 | async-start | bytes 3670016 | tf_op jit(solution)/shard_map/all_to_all | solution.py:84
  28.2 2.1 gather_fusion
  30.3 2.8 reshape.247
  33.1 3.2 %broadcast_in_dim.59 = bf16[16,2,36864]{2,1,0:T(2,128)(2,1)} broadcast(bf16[]{:T(256)} %constant.40.clone.1), dimensions={} | broadcast | bytes 2359298 | tf_op jit(solution)/shard_map/broadcast_in_dim | solution.py:61
  36.3 3.0 constant_dynamic-slice_fusion
  39.3 0.4 collective-permute-start
  39.9 9.8 %reshape.240 = bf16[4096,576]{1,0:T(8,128)(2,1)} reshape(bf16[128,18432]{1,0:T(8,128)(2,1)} %param.12) | data formatting | bytes 9437184 | tf_op jit(solution)/shard_map/reshape | solution.py:17
  50.1 1.5 collective-permute-start.2
  51.5 0.3 collective-permute-start.3
  51.8 1.5 collective-permute-start.4
  53.4 0.8 constant_dynamic-update-slice_fusion.14
  54.1 4.0 %collective-permute-done.1 = bf16[1,2,36864]{2,1,0:T(2,128)(2,1)S(1)} collective-permute-done((bf16[1,2,36864]{2,1,0:T(2,128)(2,1)S(1)}, bf16[1,2,36864]{2,1,0:T(2,128)(2,1)S(1)}, u32[]{:S(2)}, u32[]{:S(2)}) %collective-permute-start.1) | collective-permute-done | bytes 147488 | tf_op jit(solution)/shard_map/ppermute | solution.py:65
  58.1 0.8 constant_dynamic-update-slice_fusion.13
  58.9 4.8 %collective-permute-done.2 = bf16[1,2,36864]{2,1,0:T(2,128)(2,1)S(1)} collective-permute-done((bf16[1,2,36864]{2,1,0:T(2,128)(2,1)S(1)}, bf16[1,2,36864]{2,1,0:T(2,128)(2,1)S(1)}, u32[]{:S(2)}, u32[]{:S(2)}) %collective-permute-start.2) | collective-permute-done | bytes 147488 | tf_op jit(solution)/shard_map/ppermute | solution.py:65
  63.7 0.4 collective-permute-start.7
  64.1 0.8 constant_dynamic-update-slice_fusion.12
  64.9 1.9 collective-permute-start.8
  66.8 0.8 constant_dynamic-update-slice_fusion.11
  67.6 10.4 %collective-permute-start.9 = (bf16[1,2,36864]{2,1,0:T(2,128)(2,1)S(1)}, bf16[1,2,36864]{2,1,0:T(2,128)(2,1)S(1)}, u32[]{:S(2)}, u32[]{:S(2)}) collective-permute-start(bf16[1,2,36864]{2,1,0:T(2,128)(2,1)S(1)} %get-tuple-element.11), channel_id=1, source_target_pairs={{0,10},{1,11},{2,8},{3,9},{4,14},{5,15},{6,12},{7,13},{8,2},{9,3},... | collective-permute-start | bytes 442376 | tf_op jit(solution)/shard_map/ppermute | solution.py:65
  78.0 0.8 constant_dynamic-update-slice_fusion.10
  78.9 0.8 constant_dynamic-update-slice_fusion.9
  79.7 1.0 collective-permute-start.11
  80.7 0.8 constant_dynamic-update-slice_fusion.8
  81.5 0.8 collective-permute-start.12
  82.3 0.7 constant_dynamic-update-slice_fusion.7
  83.1 10.1 %collective-permute-done.8 = bf16[1,2,36864]{2,1,0:T(2,128)(2,1)S(1)} collective-permute-done((bf16[1,2,36864]{2,1,0:T(2,128)(2,1)S(1)}, bf16[1,2,36864]{2,1,0:T(2,128)(2,1)S(1)}, u32[]{:S(2)}, u32[]{:S(2)}) %collective-permute-start.8) | collective-permute-done | bytes 147488 | tf_op jit(solution)/shard_map/ppermute | solution.py:65
  93.2 0.8 constant_dynamic-update-slice_fusion.6
  93.9 2.4 collective-permute-done.9
  96.3 3.0 %collective-permute-start.14 = (bf16[1,2,36864]{2,1,0:T(2,128)(2,1)S(1)}, bf16[1,2,36864]{2,1,0:T(2,128)(2,1)S(1)}, u32[]{:S(2)}, u32[]{:S(2)}) collective-permute-start(bf16[1,2,36864]{2,1,0:T(2,128)(2,1)S(1)} %get-tuple-element.6), channel_id=1, source_target_pairs={{0,15},{1,14},{2,13},{3,12},{4,11},{5,10},{6,9},{7,8},{8,7},{9,6},... | collective-permute-start | bytes 442376 | tf_op jit(solution)/shard_map/ppermute | solution.py:65
  99.4 0.8 constant_dynamic-update-slice_fusion.5
  100.1 2.5 collective-permute-done.10
  102.6 0.8 constant_dynamic-update-slice_fusion.4
  103.4 7.2 %collective-permute-done.11 = bf16[1,2,36864]{2,1,0:T(2,128)(2,1)S(1)} collective-permute-done((bf16[1,2,36864]{2,1,0:T(2,128)(2,1)S(1)}, bf16[1,2,36864]{2,1,0:T(2,128)(2,1)S(1)}, u32[]{:S(2)}, u32[]{:S(2)}) %collective-permute-start.11) | collective-permute-done | bytes 147488 | tf_op jit(solution)/shard_map/ppermute | solution.py:65
  110.6 0.8 constant_dynamic-update-slice_fusion.3
  111.4 3.2 %collective-permute-done.12 = bf16[1,2,36864]{2,1,0:T(2,128)(2,1)S(1)} collective-permute-done((bf16[1,2,36864]{2,1,0:T(2,128)(2,1)S(1)}, bf16[1,2,36864]{2,1,0:T(2,128)(2,1)S(1)}, u32[]{:S(2)}, u32[]{:S(2)}) %collective-permute-start.12) | collective-permute-done | bytes 147488 | tf_op jit(solution)/shard_map/ppermute | solution.py:65
  114.6 0.8 constant_dynamic-update-slice_fusion.2
  115.4 2.5 reshape.243
  118.1 0.8 constant_dynamic-update-slice_fusion.1
  118.9 32.5 %all-gather.2.cloned.1.call-done = bf16[320,3584]{1,0:T(8,128)(2,1)} async-done(((bf16[160,3584]{1,0:T(8,128)(2,1)}), bf16[320,3584]{1,0:T(8,128)(2,1)}) %all-gather.2.cloned.1.call-update) | async-done | bytes 2293776 | tf_op jit(solution)/shard_map/all_gather | solution.py:91
  151.4 4.1 %fusion.7 = f32[320,512]{1,0:T(8,128)S(1)} fusion(bf16[320,3584]{1,0:T(8,128)(2,1)} %all-gather.2.cloned.1.call-done, bf16[1,3584,512]{2,1,0:T(8,128)(2,1)} %param.21), kind=kOutput, calls=%fused_computation.15 | convolution fusion | flops 1174405120 | bytes 6619136 | tf_op jit(solution)/shard_map/dot_general | solution.py:92
  155.5 8.6 %fusion.3 = f32[320,3584]{1,0:T(8,128)} fusion(bf16[1,512,3584]{2,1,0:T(8,128)(2,1)} %param.23, bf16[320,3584]{1,0:T(8,128)(2,1)} %all-gather.2.cloned.1.call-done, bf16[1,3584,512]{2,1,0:T(8,128)(2,1)} %param.22, f32[320,512]{1,0:T(8,128)S(1)} %fusion.7), kind=kOutput, calls=%fused_computation.11 | convolution fusion | flops 2349793280 | bytes 14876672 | tf_op jit(solution)/shard_map/dot_general | solution.py:96
  164.0 0.8 constant_dynamic-update-slice_fusion
  164.8 2.9 reshape.238
  167.7 3.5 %gather_fusion.1 = bf16[32,36864]{1,0:T(8,128)(2,1)} fusion(bf16[32,36864]{1,0:T(8,128)(2,1)S(1)} %reshape.238, s32[1024]{0:T(1024)S(1)} %pad_clamp_fusion.1), kind=kCustom, calls=%fused_computation.1 | custom fusion | bytes 4718720 | tf_op jit(solution)/shard_map/gather | solution.py:69
  171.2 4.7 %reshape.239 = bf16[2048,576]{1,0:T(8,128)(2,1)S(1)} reshape(bf16[32,36864]{1,0:T(8,128)(2,1)} %gather_fusion.1) | data formatting | bytes 4718592 | tf_op jit(solution)/shard_map/reshape | solution.py:69
  175.9 25.5 %fusion = (f32[4096]{0:T(1024)S(1)}, f32[2176,4096]{1,0:T(8,128)}) fusion(s32[4096]{0:T(1024)S(1)} %add_select_fusion, s32[2176]{0:T(1024)S(1)} %iota_add_fusion, pred[2176]{0:T(1024)(128)(4,1)S(1)} %get-tuple-element.24, pred[2176]{0:T(1024)(128)(4,1)S(1)} %get-tuple-element.25, bf16[4096,576]{1,0:T(8,128)(2,1)} %reshape.240, ...), kind=kOutput, calls=%fused_computation.7 | convolution fusion | flops 10317230080 | bytes 42922752 | tf_op jit(solution)/shard_map/dot_general | solution.py:20
  201.4 32.7 %fusion.41 = (f32[4096]{0:T(1024)S(1)}, f32[4096,2176]{0,1:T(8,128)}) fusion(f32[4096]{0:T(1024)S(1)} %get-tuple-element.22, f32[2176,4096]{1,0:T(8,128)} %get-tuple-element.23, s32[4096]{0:T(1024)S(1)} %add_select_fusion, s32[2176]{0:T(1024)S(1)} %iota_add_fusion, pred[2176]{0:T(1024)(128)(4,1)S(1)} %get-tuple-element.24, ...), kind=kLoop, calls=%fused_computation.103 | loop fusion | flops 62386176 | bytes 71365376 | tf_op jit(solution)/shard_map/reduce_sum | solution.py:34
  234.1 1.8 convert_element_type.30
  235.9 1.5 reshape.244
  237.3 6.7 %all-to-all-start.2 = ((bf16[16,10,3584]{2,1,0:T(8,128)(2,1)}), bf16[16,10,3584]{2,1,0:T(8,128)(2,1)}, u32[]{:S(2)}, u32[]{:S(2)}) async-start(bf16[16,10,3584]{2,1,0:T(8,128)(2,1)} %reshape.244), calls=%async_computation.3 | async-start | bytes 3670016 | tf_op jit(solution)/shard_map/all_to_all | solution.py:101
  244.1 17.7 %fusion.2 = bf16[4096,512]{1,0:T(8,128)(2,1)} fusion(f32[4096,2176]{0,1:T(8,128)} %get-tuple-element.5, f32[4096]{0:T(1024)S(1)} %get-tuple-element.4, bf16[128,576]{1,0:T(8,128)(2,1)S(1)} %copy.34, bf16[2048,576]{1,0:T(8,128)(2,1)S(1)} %copy-done.4), kind=kOutput, calls=%fused_computation.9 | convolution fusion | flops 9151184896 | bytes 42369024 | tf_op jit(solution)/shard_map/dot_general | solution.py:35
  261.7 7.4 %reshape.241 = bf16[128,16384]{1,0:T(8,128)(2,1)} reshape(bf16[4096,512]{1,0:T(8,128)(2,1)} %fusion.2) | data formatting | bytes 8388608 | tf_op jit(solution)/shard_map/reshape | solution.py:36
  269.1 16.9 %all-to-all-done.2 = bf16[16,10,3584]{2,1,0:T(8,128)(2,1)} async-done(((bf16[16,10,3584]{2,1,0:T(8,128)(2,1)}), bf16[16,10,3584]{2,1,0:T(8,128)(2,1)}, u32[]{:S(2)}, u32[]{:S(2)}) %all-to-all-start.2) | async-done | bytes 1146912 | tf_op jit(solution)/shard_map/all_to_all | solution.py:101
  286.0 1.7 reshape.245
  287.7 1.1 gather_fusion.2
  288.8 1.3 fusion.16
  (56 shorter events, 2.3 us)
Async XLA Ops:
  7.2 21.0 %copy-start = (bf16[8,36864]{1,0:T(8,128)(2,1)S(1)}, bf16[8,36864]{1,0:T(8,128)(2,1)}, u32[]{:S(2)}) copy-start(bf16[8,36864]{1,0:T(8,128)(2,1)} %param.14) | copy-start | bytes 1769476
  9.4 12.4 %all-to-all-start = ((s32[16,1,2]{2,1,0:T(1,128)}), s32[16,1,2]{2,1,0:T(1,128)S(1)}, u32[]{:S(2)}, u32[]{:S(2)}) async-start(s32[16,1,2]{2,1,0:T(1,128)} %copy.31), calls=%async_computation | async-start | bytes 16384 | tf_op jit(solution)/shard_map/all_to_all | solution.py:54
  21.8 93.6 %all-to-all-start.1 = ((bf16[16,10,3584]{2,1,0:T(8,128)(2,1)}), bf16[16,10,3584]{2,1,0:T(8,128)(2,1)}, u32[]{:S(2)}, u32[]{:S(2)}) async-start(bf16[16,10,3584]{2,1,0:T(8,128)(2,1)} %reshape.242), calls=%async_computation.1 | async-start | bytes 3670016 | tf_op jit(solution)/shard_map/all_to_all | solution.py:84
  27.8 123.5 %all-gather.2.cloned.1.call-start = ((), (), s32[]{:S(2)}) async-start(), calls=%async_computation.4 | async-start | bytes 3440640 | tf_op jit(solution)/shard_map/all_gather | solution.py:91
  33.1 3.2 %copy-start.2 = (bf16[16,2,36864]{2,1,0:T(2,128)(2,1)S(1)}, bf16[16,2,36864]{2,1,0:T(2,128)(2,1)}, u32[]{:S(2)}) copy-start(bf16[16,2,36864]{2,1,0:T(2,128)(2,1)} %reshape.247) | copy-start | bytes 7077892
  36.3 3.4 %copy-start.5 = (bf16[128,576]{0,1:T(8,128)(2,1)S(1)}, bf16[128,576]{0,1:T(8,128)(2,1)}, u32[]{:S(2)}) copy-start(bf16[128,576]{0,1:T(8,128)(2,1)} %param.13) | copy-start | bytes 442372
  39.3 14.0 %collective-permute-start = (bf16[1,2,36864]{2,1,0:T(2,128)(2,1)S(1)}, bf16[1,2,36864]{2,1,0:T(2,128)(2,1)S(1)}, u32[]{:S(2)}, u32[]{:S(2)}) collective-permute-start(bf16[1,2,36864]{2,1,0:T(2,128)(2,1)S(1)} %get-tuple-element.20), channel_id=1, source_target_pairs={{0,1},{1,0},{2,3},{3,2},{4,5},{5,4},{6,7},{7,6},{8,9},{9,8},{10,11... | collective-permute-start | bytes 442376 | tf_op jit(solution)/shard_map/ppermute | solution.py:65
  39.8 9.8 %copy-start.6 = (f32[16,8]{0,1:T(8,128)S(1)}, f32[16,8]{0,1:T(8,128)}, u32[]{:S(2)}) copy-start(f32[16,8]{0,1:T(8,128)} %param.20) | copy-start | bytes 1540
  49.8 8.4 %collective-permute-start.1 = (bf16[1,2,36864]{2,1,0:T(2,128)(2,1)S(1)}, bf16[1,2,36864]{2,1,0:T(2,128)(2,1)S(1)}, u32[]{:S(2)}, u32[]{:S(2)}) collective-permute-start(bf16[1,2,36864]{2,1,0:T(2,128)(2,1)S(1)} %get-tuple-element.19), channel_id=1, source_target_pairs={{0,2},{1,3},{2,0},{3,1},{4,6},{5,7},{6,4},{7,5},{8,10},{9,11},{10,... | collective-permute-start | bytes 442376 | tf_op jit(solution)/shard_map/ppermute | solution.py:65
  50.1 13.7 %collective-permute-start.2 = (bf16[1,2,36864]{2,1,0:T(2,128)(2,1)S(1)}, bf16[1,2,36864]{2,1,0:T(2,128)(2,1)S(1)}, u32[]{:S(2)}, u32[]{:S(2)}) collective-permute-start(bf16[1,2,36864]{2,1,0:T(2,128)(2,1)S(1)} %get-tuple-element.18), channel_id=1, source_target_pairs={{0,3},{1,2},{2,1},{3,0},{4,7},{5,6},{6,5},{7,4},{8,11},{9,10},{10,... | collective-permute-start | bytes 442376 | tf_op jit(solution)/shard_map/ppermute | solution.py:65
  51.5 13.4 %collective-permute-start.3 = (bf16[1,2,36864]{2,1,0:T(2,128)(2,1)S(1)}, bf16[1,2,36864]{2,1,0:T(2,128)(2,1)S(1)}, u32[]{:S(2)}, u32[]{:S(2)}) collective-permute-start(bf16[1,2,36864]{2,1,0:T(2,128)(2,1)S(1)} %get-tuple-element.17), channel_id=1, source_target_pairs={{0,4},{1,5},{2,6},{3,7},{4,0},{5,1},{6,2},{7,3},{8,12},{9,13},{10,... | collective-permute-start | bytes 442376 | tf_op jit(solution)/shard_map/ppermute | solution.py:65
  51.8 15.8 %collective-permute-start.4 = (bf16[1,2,36864]{2,1,0:T(2,128)(2,1)S(1)}, bf16[1,2,36864]{2,1,0:T(2,128)(2,1)S(1)}, u32[]{:S(2)}, u32[]{:S(2)}) collective-permute-start(bf16[1,2,36864]{2,1,0:T(2,128)(2,1)S(1)} %get-tuple-element.16), channel_id=1, source_target_pairs={{0,5},{1,4},{2,7},{3,6},{4,1},{5,0},{6,3},{7,2},{8,13},{9,12},{10,... | collective-permute-start | bytes 442376 | tf_op jit(solution)/shard_map/ppermute | solution.py:65
  53.3 25.5 %collective-permute-start.5 = (bf16[1,2,36864]{2,1,0:T(2,128)(2,1)S(1)}, bf16[1,2,36864]{2,1,0:T(2,128)(2,1)S(1)}, u32[]{:S(2)}, u32[]{:S(2)}) collective-permute-start(bf16[1,2,36864]{2,1,0:T(2,128)(2,1)S(1)} %get-tuple-element.15), channel_id=1, source_target_pairs={{0,6},{1,7},{2,4},{3,5},{4,2},{5,3},{6,0},{7,1},{8,14},{9,15},{10,... | collective-permute-start | bytes 442376 | tf_op jit(solution)/shard_map/ppermute | solution.py:65
  58.1 21.6 %collective-permute-start.6 = (bf16[1,2,36864]{2,1,0:T(2,128)(2,1)S(1)}, bf16[1,2,36864]{2,1,0:T(2,128)(2,1)S(1)}, u32[]{:S(2)}, u32[]{:S(2)}) collective-permute-start(bf16[1,2,36864]{2,1,0:T(2,128)(2,1)S(1)} %get-tuple-element.14), channel_id=1, source_target_pairs={{0,7},{1,6},{2,5},{3,4},{4,3},{5,2},{6,1},{7,0},{8,15},{9,14},{10,... | collective-permute-start | bytes 442376 | tf_op jit(solution)/shard_map/ppermute | solution.py:65
  63.7 17.8 %collective-permute-start.7 = (bf16[1,2,36864]{2,1,0:T(2,128)(2,1)S(1)}, bf16[1,2,36864]{2,1,0:T(2,128)(2,1)S(1)}, u32[]{:S(2)}, u32[]{:S(2)}) collective-permute-start(bf16[1,2,36864]{2,1,0:T(2,128)(2,1)S(1)} %get-tuple-element.13), channel_id=1, source_target_pairs={{0,8},{1,9},{2,10},{3,11},{4,12},{5,13},{6,14},{7,15},{8,0},{9,1},... | collective-permute-start | bytes 442376 | tf_op jit(solution)/shard_map/ppermute | solution.py:65
  64.9 28.3 %collective-permute-start.8 = (bf16[1,2,36864]{2,1,0:T(2,128)(2,1)S(1)}, bf16[1,2,36864]{2,1,0:T(2,128)(2,1)S(1)}, u32[]{:S(2)}, u32[]{:S(2)}) collective-permute-start(bf16[1,2,36864]{2,1,0:T(2,128)(2,1)S(1)} %get-tuple-element.12), channel_id=1, source_target_pairs={{0,9},{1,8},{2,11},{3,10},{4,13},{5,12},{6,15},{7,14},{8,1},{9,0},... | collective-permute-start | bytes 442376 | tf_op jit(solution)/shard_map/ppermute | solution.py:65
  67.6 28.7 %collective-permute-start.9 = (bf16[1,2,36864]{2,1,0:T(2,128)(2,1)S(1)}, bf16[1,2,36864]{2,1,0:T(2,128)(2,1)S(1)}, u32[]{:S(2)}, u32[]{:S(2)}) collective-permute-start(bf16[1,2,36864]{2,1,0:T(2,128)(2,1)S(1)} %get-tuple-element.11), channel_id=1, source_target_pairs={{0,10},{1,11},{2,8},{3,9},{4,14},{5,15},{6,12},{7,13},{8,2},{9,3},... | collective-permute-start | bytes 442376 | tf_op jit(solution)/shard_map/ppermute | solution.py:65
  78.8 23.9 %collective-permute-start.10 = (bf16[1,2,36864]{2,1,0:T(2,128)(2,1)S(1)}, bf16[1,2,36864]{2,1,0:T(2,128)(2,1)S(1)}, u32[]{:S(2)}, u32[]{:S(2)}) collective-permute-start(bf16[1,2,36864]{2,1,0:T(2,128)(2,1)S(1)} %get-tuple-element.10), channel_id=1, source_target_pairs={{0,11},{1,10},{2,9},{3,8},{4,15},{5,14},{6,13},{7,12},{8,3},{9,2},... | collective-permute-start | bytes 442376 | tf_op jit(solution)/shard_map/ppermute | solution.py:65
  79.7 30.9 %collective-permute-start.11 = (bf16[1,2,36864]{2,1,0:T(2,128)(2,1)S(1)}, bf16[1,2,36864]{2,1,0:T(2,128)(2,1)S(1)}, u32[]{:S(2)}, u32[]{:S(2)}) collective-permute-start(bf16[1,2,36864]{2,1,0:T(2,128)(2,1)S(1)} %get-tuple-element.9), channel_id=1, source_target_pairs={{0,12},{1,13},{2,14},{3,15},{4,8},{5,9},{6,10},{7,11},{8,4},{9,5},... | collective-permute-start | bytes 442376 | tf_op jit(solution)/shard_map/ppermute | solution.py:65
  81.5 33.1 %collective-permute-start.12 = (bf16[1,2,36864]{2,1,0:T(2,128)(2,1)S(1)}, bf16[1,2,36864]{2,1,0:T(2,128)(2,1)S(1)}, u32[]{:S(2)}, u32[]{:S(2)}) collective-permute-start(bf16[1,2,36864]{2,1,0:T(2,128)(2,1)S(1)} %get-tuple-element.8), channel_id=1, source_target_pairs={{0,13},{1,12},{2,15},{3,14},{4,9},{5,8},{6,11},{7,10},{8,5},{9,4},... | collective-permute-start | bytes 442376 | tf_op jit(solution)/shard_map/ppermute | solution.py:65
  93.2 24.9 %collective-permute-start.13 = (bf16[1,2,36864]{2,1,0:T(2,128)(2,1)S(1)}, bf16[1,2,36864]{2,1,0:T(2,128)(2,1)S(1)}, u32[]{:S(2)}, u32[]{:S(2)}) collective-permute-start(bf16[1,2,36864]{2,1,0:T(2,128)(2,1)S(1)} %get-tuple-element.7), channel_id=1, source_target_pairs={{0,14},{1,15},{2,12},{3,13},{4,10},{5,11},{6,8},{7,9},{8,6},{9,7},... | collective-permute-start | bytes 442376 | tf_op jit(solution)/shard_map/ppermute | solution.py:65
  96.3 67.7 %collective-permute-start.14 = (bf16[1,2,36864]{2,1,0:T(2,128)(2,1)S(1)}, bf16[1,2,36864]{2,1,0:T(2,128)(2,1)S(1)}, u32[]{:S(2)}, u32[]{:S(2)}) collective-permute-start(bf16[1,2,36864]{2,1,0:T(2,128)(2,1)S(1)} %get-tuple-element.6), channel_id=1, source_target_pairs={{0,15},{1,14},{2,13},{3,12},{4,11},{5,10},{6,9},{7,8},{8,7},{9,6},... | collective-permute-start | bytes 442376 | tf_op jit(solution)/shard_map/ppermute | solution.py:65
  117.9 116.2 %reduce-scatter.2.cloned.1.call-start = ((), (), s32[]{:S(2)}) async-start(), calls=%async_computation.5 | async-start | bytes 6881280 | tf_op jit(solution)/shard_map/reduce_scatter | solution.py:95
  175.9 25.5 %copy-start.3 = (bf16[2048,576]{1,0:T(8,128)(2,1)}, bf16[2048,576]{1,0:T(8,128)(2,1)S(1)}, u32[]{:S(2)}) copy-start(bf16[2048,576]{1,0:T(8,128)(2,1)S(1)} %reshape.239) | copy-start | bytes 7077892
  237.3 6.7 %copy-start.4 = (bf16[2048,576]{1,0:T(8,128)(2,1)S(1)}, bf16[2048,576]{1,0:T(8,128)(2,1)}, u32[]{:S(2)}) copy-start(bf16[2048,576]{1,0:T(8,128)(2,1)} %copy-done.3) | copy-start | bytes 7077892
  237.3 48.6 %all-to-all-start.2 = ((bf16[16,10,3584]{2,1,0:T(8,128)(2,1)}), bf16[16,10,3584]{2,1,0:T(8,128)(2,1)}, u32[]{:S(2)}, u32[]{:S(2)}) async-start(bf16[16,10,3584]{2,1,0:T(8,128)(2,1)} %reshape.244), calls=%async_computation.3 | async-start | bytes 3670016 | tf_op jit(solution)/shard_map/all_to_all | solution.py:101
  287.6 2.5 copy-start.1
Sparse Core Ops, SparseCore 0:
  118.0 33.3 all-gather.1
  164.2 58.6 reduce-scatter.1
